TPU v7x, 512 devices: a whole 4x8x8 slice. The times are simulated.
512 devices in a mesh: rep: 32 (over z, y_hi), sp: 16 (over y_lo, x, core).
Axes of the slice: x: 4, y: 8 (y_hi: 4, y_lo: 2; y = y_hi * 2 + y_lo), z: 8, core: 2. Of those that a mesh axis runs over, the one named last changes fastest.
Arguments:
- queries: bfloat16 [32, 3072, 2048], P('rep', 'sp'), may hold values from -13 to 13
- key_rows: bfloat16 [32, 3072, 2048], P('rep', 'sp'), may hold values from -13 to 13
- values: bfloat16 [32, 3072, 2048], P('rep', 'sp'), may hold values from -6 to 6
- out_grad: bfloat16 [32, 3072, 3072], P('rep', 'sp'), may hold values from -6 to 6
- clip_count: int32 [32], P('rep'), may hold values from 1 to 3, as said below
- clip_lengths: int32 [32, 3], P('rep'), may hold values from 0 to 3072, as said below
- adapter_in: float32 [2048, 128], P('sp'), may hold values from -4 to 4
- adapter_out: float32 [128, 3072], P('sp'), may hold values from -4 to 4
- moment_in: float32 [2048, 128], P('sp'), may hold values from -3 to 3
- square_in: float32 [2048, 128], P('sp'), may hold values from 0.05 to 2
- moment_out: float32 [128, 3072], P('sp'), may hold values from -3 to 3
- square_out: float32 [128, 3072], P('sp'), may hold values from 0.05 to 2
Outputs:
- momentum_in: float32 [2048, 128], P('sp')
- variance_in: float32 [2048, 128], P('sp')
- update_in: float32 [2048, 128], P('sp')
- momentum_out: float32 [128, 3072], P('sp')
- variance_out: float32 [128, 3072], P('sp')
- update_out: float32 [128, 3072], P('sp')
Inputs may be any that keep to these rules, and one draw needn't show every extreme that they name: `clip_count`: in every draw some replica has 1 clip and some replica has 3. `clip_lengths`: each entry is a multiple of 384; entries at or beyond a replica's clip count are 0, the others 384 or more; the entries of a replica sum to at most 3072, and in every draw some replica holds a single clip of exactly 3072.
All inputs are finite; a program needn't handle non-finite values.
Results may differ from a plain program's by a relative error of at most 0.0017.
Values may be sent and summed in bfloat16 or wider, within the bound.
A program may use at most 64 MiB of HBM per device.

v0:
```python
import math
import jax
import jax.numpy as jnp
from jax import lax
from jax.sharding import PartitionSpec as P

HD = 128
MAX_CLIPS = 3
first_rate = 0.9
second_rate = 0.999
adam_steps = 100.0
adam_epsilon = 1e-08
decay_rate = 0.1


def laid_out(blocks, dim):
    shape = list(blocks.shape[1:])
    shape[dim] *= blocks.shape[0]
    return jnp.moveaxis(blocks, 0, dim).reshape(shape)


def gather_packed(arrays, axis, dims):
    ravelled = jnp.concatenate([a.reshape(-1) for a in arrays])
    lines, at, done = (lax.all_gather(ravelled, axis), 0, [])
    for a, dim in zip(arrays, dims):
        blocks = lines[:, at : at + a.size].reshape(-1, *a.shape)
        done.append(laid_out(blocks, dim))
        at += a.size
    return tuple(done)


def cut_along(array, dim, peers):
    shape = array.shape
    blocks = array.reshape(*shape[:dim], peers, shape[dim] // peers, *shape[dim + 1 :])
    return jnp.moveaxis(blocks, dim, 0)


def sum_packed(arrays, axis, dims):
    peers = lax.axis_size(axis)
    blocks = [cut_along(a, dim, peers) for a, dim in zip(arrays, dims)]
    lines = jnp.concatenate([b.reshape(peers, -1) for b in blocks], axis=1)
    extent = max(16, -(-lines.shape[1] // 1024) * 8)
    lines = jnp.pad(lines, ((0, 0), (0, extent * 128 - lines.shape[1]))).reshape(-1, 128)
    ravelled, at, done = (lax.psum_scatter(lines, axis, tiled=True).reshape(-1), 0, [])
    for b in blocks:
        part = b[0]
        done.append(ravelled[at : at + part.size].reshape(part.shape))
        at += part.size
    return tuple(done)


def padded_to(lines, peers):
    spare = -lines.shape[0] % peers
    if not spare:
        return lines
    return jnp.concatenate([lines, jnp.zeros((spare, *lines.shape[1:]), lines.dtype)])


def sent_to_all(array, axis):
    peers = lax.axis_size(axis)
    return lax.all_to_all(
        jnp.broadcast_to(array[None], (peers, *array.shape)), axis, 0, 0, tiled=True
    )


def gathered_copies(array, axis, dim):
    return laid_out(sent_to_all(array, axis), dim)


def summed_on_arrival(array, axis, dim):
    blocks = cut_along(array, dim, lax.axis_size(axis))
    arrived = lax.all_to_all(blocks, axis, split_axis=0, concat_axis=0, tiled=True)
    return arrived.sum(axis=0)


def total_of(array, axes):
    padded = padded_to(array, lax.axis_size(axes))
    whole = gathered_copies(summed_on_arrival(padded, axes, 0), axes, 0)
    return lax.slice_in_dim(whole, 0, len(array)).reshape(array.shape)


def packed_total(arrays, axis):
    ends = [0]
    for a in arrays:
        ends.append(ends[-1] + a.size)
    total = total_of(jnp.concatenate([a.ravel() for a in arrays]), axis)
    return tuple((total[b:e].reshape(a.shape) for a, b, e in zip(arrays, ends, ends[1:])))


def segment_ids(count, lengths, positions):
    active = (jnp.arange(lengths.shape[0], dtype=jnp.int32) < count).astype(lengths.dtype)
    ends = jnp.cumsum(lengths * active)
    return jnp.sum((positions[:, None] >= ends[None, :]).astype(jnp.int32), axis=1)


def adamw(param, grad, moment, square):
    momentum = first_rate * moment + (1.0 - first_rate) * grad
    variance = second_rate * square + (1.0 - second_rate) * grad * grad
    first_hat = momentum / (1.0 - first_rate**adam_steps)
    second_hat = variance / (1.0 - second_rate**adam_steps)
    update = first_hat / (jnp.sqrt(second_hat) + adam_epsilon) + decay_rate * param
    return (momentum, variance, update)


def contract_rows(left, right):
    return lax.dot_general(
        left, right, (((0,), (0,)), ((), ())), preferred_element_type=jnp.float32
    )


def per_device(
    queries,
    key_rows,
    values,
    out_grad,
    clip_count,
    clip_lengths,
    adapter_in,
    adapter_out,
    moment_in,
    square_in,
    moment_out,
    square_out,
):
    tok_dev = queries.shape[1]
    inner = queries.shape[2]
    rank = adapter_in.shape[1]
    groups = lax.axis_size("sp")
    tokens = tok_dev * groups
    heads = inner // HD
    head_share = heads // groups
    positions = jnp.arange(tokens, dtype=jnp.int32)
    segment = segment_ids(clip_count[0], clip_lengths[0], positions)
    segment_mine = lax.dynamic_slice_in_dim(segment, lax.axis_index("sp") * tok_dev, tok_dev)
    live = (segment_mine < MAX_CLIPS).astype(out_grad.dtype)
    grad_live = out_grad[0] * live[:, None]
    block = math.gcd(512, tokens)
    blocks = tokens // block

    def attend_head(query_head, key_head, value_head):

        def one_block(pair):
            query_block, segment_block = pair
            scores = lax.dot_general(
                query_block, key_head, (((1,), (1,)), ((), ())), preferred_element_type=jnp.float32
            ) * HD ** (-0.5)
            allowed = segment_block[:, None] == segment[None, :]
            highest = jnp.max(jnp.where(allowed, scores, -jnp.inf), axis=1, keepdims=True)
            exponent = jnp.exp(jnp.where(allowed, scores - highest, -jnp.inf))
            row_total = jnp.sum(exponent, axis=1, keepdims=True)
            weights = exponent.astype(jnp.bfloat16)
            mixed = jnp.dot(weights, value_head, preferred_element_type=jnp.float32) / row_total
            return mixed.astype(jnp.bfloat16)

        result = lax.map(
            one_block, (query_head.reshape(blocks, block, HD), segment.reshape(blocks, block))
        )
        return result.reshape(tokens, HD)

    query_split = queries.reshape(tok_dev, groups, head_share, HD)
    key_split = key_rows.reshape(tok_dev, groups, head_share, HD)
    value_split = values.reshape(tok_dev, groups, head_share, HD)
    query_part = lax.all_to_all(query_split, "sp", split_axis=1, concat_axis=0, tiled=True)
    key_part = lax.all_to_all(key_split, "sp", split_axis=1, concat_axis=0, tiled=True)
    value_part = lax.all_to_all(value_split, "sp", split_axis=1, concat_axis=0, tiled=True)
    per_head = jax.vmap(attend_head, in_axes=1, out_axes=1)
    mixed = per_head(query_part[:, 0], key_part[:, 0], value_part[:, 0])[:, None]
    returned = lax.all_to_all(mixed, "sp", split_axis=0, concat_axis=1, tiled=True)
    attended = returned.reshape(tok_dev, inner)
    inner_all, outer_all = gather_packed(
        (adapter_in.astype(jnp.bfloat16), adapter_out.astype(jnp.bfloat16)), "sp", (0, 0)
    )
    adapted = (
        jnp.dot(attended, inner_all, preferred_element_type=jnp.float32) * inner ** (-0.5)
    ).astype(jnp.bfloat16)
    slopes = (
        lax.dot_general(
            grad_live, outer_all, (((1,), (1,)), ((), ())), preferred_element_type=jnp.float32
        )
        * rank ** (-0.5)
    ).astype(jnp.bfloat16)
    term_in = contract_rows(attended, slopes) * inner ** (-0.5)
    term_out = contract_rows(adapted, grad_live) * rank ** (-0.5)
    grad_in, grad_out = sum_packed((term_in, term_out), "sp", (0, 0))
    grad_in, grad_out = packed_total((grad_in, grad_out), "rep")
    momentum_in, variance_in, update_in = adamw(adapter_in, grad_in, moment_in, square_in)
    momentum_out, variance_out, update_out = adamw(adapter_out, grad_out, moment_out, square_out)
    return (momentum_in, variance_in, update_in, momentum_out, variance_out, update_out)


def solution(mesh):
    placed = (
        P("rep", "sp", None),
        P("rep", "sp", None),
        P("rep", "sp", None),
        P("rep", "sp", None),
        P("rep"),
        P("rep", None),
        P("sp", None),
        P("sp", None),
        P("sp", None),
        P("sp", None),
        P("sp", None),
        P("sp", None),
    )
    return jax.shard_map(
        per_device,
        mesh=mesh,
        in_specs=placed,
        out_specs=(
            P("sp", None),
            P("sp", None),
            P("sp", None),
            P("sp", None),
            P("sp", None),
            P("sp", None),
        ),
        check_vma=False,
    )
```

profile of v0, /device:TPU:8, one launch (start us, length us, event | category | flops | bytes accessed | tf_op | source)
XLA Modules:
  0.0 250.4 jit_solution(16553010181526871349)
XLA Ops:
  7.2 1.4 copy.51
  8.5 1.1 copy.42
  9.7 9.4 %all-to-all-start = ((bf16[192,16,1,128]{3,0,2,1:T(8,128)(2,1)}), bf16[192,16,1,128]{3,0,2,1:T(8,128)(2,1)S(1)}, u32[]{:S(2)}, u32[]{:S(2)}) async-start(bf16[192,16,1,128]{3,0,2,1:T(8,128)(2,1)} %copy.42), calls=%async_computation | async-start | bytes 1572864 | tf_op jit(solution)/shard_map/all_to_all | solution.py:163
  19.2 1.1 copy.43
  20.3 11.0 %all-to-all-done = bf16[192,16,1,128]{3,0,2,1:T(8,128)(2,1)S(1)} async-done(((bf16[192,16,1,128]{3,0,2,1:T(8,128)(2,1)}), bf16[192,16,1,128]{3,0,2,1:T(8,128)(2,1)S(1)}, u32[]{:S(2)}, u32[]{:S(2)}) %all-to-all-start) | async-done | bytes 786464 | tf_op jit(solution)/shard_map/all_to_all | solution.py:163
  31.3 5.0 %all-to-all-start.1 = ((bf16[192,16,1,128]{3,0,2,1:T(8,128)(2,1)}), bf16[192,16,1,128]{3,0,2,1:T(8,128)(2,1)S(1)}, u32[]{:S(2)}, u32[]{:S(2)}) async-start(bf16[192,16,1,128]{3,0,2,1:T(8,128)(2,1)} %copy.43), calls=%async_computation.1 | async-start | bytes 1572864 | tf_op jit(solution)/shard_map/all_to_all | solution.py:164
  36.5 1.1 copy.44
  37.6 11.0 %all-to-all-done.1 = bf16[192,16,1,128]{3,0,2,1:T(8,128)(2,1)S(1)} async-done(((bf16[192,16,1,128]{3,0,2,1:T(8,128)(2,1)}), bf16[192,16,1,128]{3,0,2,1:T(8,128)(2,1)S(1)}, u32[]{:S(2)}, u32[]{:S(2)}) %all-to-all-start.1) | async-done | bytes 786464 | tf_op jit(solution)/shard_map/all_to_all | solution.py:164
  48.7 5.0 %all-to-all-start.2 = ((bf16[192,16,1,128]{3,0,2,1:T(8,128)(2,1)}), bf16[192,16,1,128]{3,0,2,1:T(8,128)(2,1)S(1)}, u32[]{:S(2)}, u32[]{:S(2)}) async-start(bf16[192,16,1,128]{3,0,2,1:T(8,128)(2,1)} %copy.44), calls=%async_computation.2 | async-start | bytes 1572864 | tf_op jit(solution)/shard_map/all_to_all | solution.py:165
  55.4 10.5 %all-to-all-done.2 = bf16[192,16,1,128]{3,0,2,1:T(8,128)(2,1)S(1)} async-done(((bf16[192,16,1,128]{3,0,2,1:T(8,128)(2,1)}), bf16[192,16,1,128]{3,0,2,1:T(8,128)(2,1)S(1)}, u32[]{:S(2)}, u32[]{:S(2)}) %all-to-all-start.2) | async-done | bytes 786464 | tf_op jit(solution)/shard_map/all_to_all | solution.py:165
  66.0 31.9 %while.10 = (s32[]{:T(128)}, bf16[6,1,512,128]{3,2,1,0:T(8,128)(2,1)S(1)}, s32[6,512]{1,0:T(8,128)S(1)}, s32[3072]{0:T(1024)S(1)}, bf16[6,1,512,128]{3,2,1,0:T(8...) while((s32[]{:T(128)}, ...), condition=%wide.region_5.6_spmd, body=%wide.region_2.5_spmd.sunk | while | flops 827456512 | bytes 20766816 | solution.py:155
  66.0 1.2 fusion.65
  67.2 1.9 fusion.66
  69.0 2.2 fusion.67
  71.3 1.2 fusion.65
  72.5 1.9 fusion.66
  74.3 2.2 fusion.67
  76.6 1.2 fusion.65
  77.8 1.9 fusion.66
  79.7 2.2 fusion.67
  81.9 1.2 fusion.65
  83.1 1.9 fusion.66
  85.0 2.2 fusion.67
  87.2 1.2 fusion.65
  88.4 1.9 fusion.66
  90.3 2.2 fusion.67
  92.5 1.2 fusion.65
  93.7 1.9 fusion.66
  95.6 2.2 fusion.67
  98.3 1.2 reduce.5
  99.6 1.1 reshape.153
  100.7 5.0 %all-to-all-start.3 = ((bf16[16,2,12288]{2,1,0:T(2,128)(2,1)}), bf16[16,2,12288]{2,1,0:T(2,128)(2,1)S(1)}, u32[]{:S(2)}, u32[]{:S(2)}) async-start(bf16[16,2,12288]{2,1,0:T(2,128)(2,1)} %reshape.153), calls=%async_computation.3 | async-start | bytes 1572864 | tf_op jit(solution)/shard_map/all_to_all | solution.py:168
  105.8 1.7 reshape.152
  107.8 1.2 reshape_reshape.12
  109.1 8.9 %all-to-all-done.3 = bf16[16,2,12288]{2,1,0:T(2,128)(2,1)S(1)} async-done(((bf16[16,2,12288]{2,1,0:T(2,128)(2,1)}), bf16[16,2,12288]{2,1,0:T(2,128)(2,1)S(1)}, u32[]{:S(2)}, u32[]{:S(2)}) %all-to-all-start.3) | async-done | bytes 786464 | tf_op jit(solution)/shard_map/all_to_all | solution.py:168
  118.0 0.7 reshape.154
  119.4 2.0 convolution_multiply_fusion
  121.4 1.4 reshape_reshape.15
  122.8 2.9 %convolution_multiply_fusion.1 = f32[2048,128]{1,0:T(8,128)S(1)} fusion(bf16[128,3072]{1,0:T(8,128)(2,1)} %reshape_reshape.12, bf16[1,192,3072]{2,1,0:T(8,128)(2,1)} %param.17, bf16[24,8,16,128]{3,2,1,0:T(8,128)(2,1)S(1)} %bitcast.105, bf16[192]{0:T(256)(128)(2,1)S(1)} %compare_convert_fusion), kind=kOutput, calls=%fused_computation.22 | convolution fusion | flops 252559360 | bytes 3801472 | tf_op jit(solution)/shard_map/dot_general | solution.py:106
  125.8 1.2 reshape_reshape.13
  126.9 1.9 pad_maximum_fusion
  128.8 1.7 reshape.149
  130.6 68.7 %reduce-scatter.2.cloned.1.call-done = f32[320,128]{1,0:T(8,128)} async-done(((f32[5120,128]{1,0:T(8,128)}), f32[320,128]{1,0:T(8,128)}) %reduce-scatter.2.cloned.1.call-update) | async-done | bytes 163856 | tf_op jit(solution)/shard_map/reduce_scatter | solution.py:44
  199.2 0.9 slice_bitcast_fusion
  200.1 0.8 slice_bitcast_fusion.1
  201.0 24.9 %all_to_all.75 = f32[32,1,1280]{2,1,0:T(1,128)S(1)} all-to-all(f32[32,1,1280]{2,1,0:T(1,128)S(1)} %bitcast.119), channel_id=1, replica_groups=mesh['rep'=32,'sp'=16] {'rep'}, dimensions={0} | all-to-all | bytes 327680 | tf_op jit(solution)/shard_map/all_to_all | solution.py:72
  226.1 15.9 %all_to_all.76 = f32[32,1,1280]{2,1,0:T(1,128)S(1)} all-to-all(f32[32,1,1280]{2,1,0:T(1,128)S(1)} %broadcast_in_dim.21), channel_id=1, replica_groups=mesh['rep'=32,'sp'=16] {'rep'}, dimensions={0} | all-to-all | bytes 327680 | tf_op jit(solution)/shard_map/all_to_all | solution.py:61
  242.1 0.7 multiply_add_fusion
  (55 shorter events, 3.9 us)
Async XLA Ops:
  7.2 11.9 %copy-start = (bf16[1,192,2048]{2,1,0:T(8,128)(2,1)S(1)}, bf16[1,192,2048]{2,1,0:T(8,128)(2,1)}, u32[]{:S(2)}) copy-start(bf16[1,192,2048]{2,1,0:T(8,128)(2,1)} %param.15) | copy-start | bytes 2359300
  9.7 26.7 %copy-start.1 = (bf16[1,192,2048]{2,1,0:T(8,128)(2,1)S(1)}, bf16[1,192,2048]{2,1,0:T(8,128)(2,1)}, u32[]{:S(2)}) copy-start(bf16[1,192,2048]{2,1,0:T(8,128)(2,1)} %param.16) | copy-start | bytes 2359300
  9.7 21.7 %all-to-all-start = ((bf16[192,16,1,128]{3,0,2,1:T(8,128)(2,1)}), bf16[192,16,1,128]{3,0,2,1:T(8,128)(2,1)S(1)}, u32[]{:S(2)}, u32[]{:S(2)}) async-start(bf16[192,16,1,128]{3,0,2,1:T(8,128)(2,1)} %copy.42), calls=%async_computation | async-start | bytes 1572864 | tf_op jit(solution)/shard_map/all_to_all | solution.py:163
  20.3 33.4 %copy-start.2 = (f32[8,3072]{1,0:T(8,128)S(1)}, f32[8,3072]{1,0:T(8,128)}, u32[]{:S(2)}) copy-start(f32[8,3072]{1,0:T(8,128)} %param.21) | copy-start | bytes 294916
  20.3 33.5 %copy-start.3 = (f32[128,128]{1,0:T(8,128)S(1)}, f32[128,128]{1,0:T(8,128)}, u32[]{:S(2)}) copy-start(f32[128,128]{1,0:T(8,128)} %param.20) | copy-start | bytes 196612
  20.3 34.8 %copy-start.9 = (s32[1,3]{1,0:T(1,128)S(1)}, s32[1,3]{1,0:T(1,128)}, u32[]{:S(2)}) copy-start(s32[1,3]{1,0:T(1,128)} %param.19) | copy-start | bytes 40
  31.3 17.3 %all-to-all-start.1 = ((bf16[192,16,1,128]{3,0,2,1:T(8,128)(2,1)}), bf16[192,16,1,128]{3,0,2,1:T(8,128)(2,1)S(1)}, u32[]{:S(2)}, u32[]{:S(2)}) async-start(bf16[192,16,1,128]{3,0,2,1:T(8,128)(2,1)} %copy.43), calls=%async_computation.1 | async-start | bytes 1572864 | tf_op jit(solution)/shard_map/all_to_all | solution.py:164
  48.7 17.3 %all-to-all-start.2 = ((bf16[192,16,1,128]{3,0,2,1:T(8,128)(2,1)}), bf16[192,16,1,128]{3,0,2,1:T(8,128)(2,1)S(1)}, u32[]{:S(2)}, u32[]{:S(2)}) async-start(bf16[192,16,1,128]{3,0,2,1:T(8,128)(2,1)} %copy.44), calls=%async_computation.2 | async-start | bytes 1572864 | tf_op jit(solution)/shard_map/all_to_all | solution.py:165
  53.7 52.1 %all-gather.3.cloned.1.call-start = ((), (), s32[]{:S(2)}) async-start(), calls=%async_computation.8 | async-start | bytes 1392640 | tf_op jit(solution)/shard_map/all_gather | solution.py:24
  100.7 17.3 %all-to-all-start.3 = ((bf16[16,2,12288]{2,1,0:T(2,128)(2,1)}), bf16[16,2,12288]{2,1,0:T(2,128)(2,1)S(1)}, u32[]{:S(2)}, u32[]{:S(2)}) async-start(bf16[16,2,12288]{2,1,0:T(2,128)(2,1)} %reshape.153), calls=%async_computation.3 | async-start | bytes 1572864 | tf_op jit(solution)/shard_map/all_to_all | solution.py:168
  105.7 93.6 %reduce-scatter.2.cloned.1.call-start = ((), (), s32[]{:S(2)}) async-start(), calls=%async_computation.7 | async-start | bytes 2785280 | tf_op jit(solution)/shard_map/reduce_scatter | solution.py:44
  130.5 111.6 %copy-start.5 = (f32[8,3072]{1,0:T(8,128)S(1)}, f32[8,3072]{1,0:T(8,128)}, u32[]{:S(2)}) copy-start(f32[8,3072]{1,0:T(8,128)} %param.25) | copy-start | bytes 294916
  130.5 111.6 %copy-start.6 = (f32[8,3072]{1,0:T(8,128)S(1)}, f32[8,3072]{1,0:T(8,128)}, u32[]{:S(2)}) copy-start(f32[8,3072]{1,0:T(8,128)} %param.24) | copy-start | bytes 294916
  130.5 112.3 %copy-start.4 = (f32[128,128]{1,0:T(8,128)S(1)}, f32[128,128]{1,0:T(8,128)}, u32[]{:S(2)}) copy-start(f32[128,128]{1,0:T(8,128)} %param.20) | copy-start | bytes 196612
  130.5 112.3 %copy-start.7 = (f32[128,128]{1,0:T(8,128)S(1)}, f32[128,128]{1,0:T(8,128)}, u32[]{:S(2)}) copy-start(f32[128,128]{1,0:T(8,128)} %param.23) | copy-start | bytes 196612
  130.5 112.3 %copy-start.8 = (f32[128,128]{1,0:T(8,128)S(1)}, f32[128,128]{1,0:T(8,128)}, u32[]{:S(2)}) copy-start(f32[128,128]{1,0:T(8,128)} %param.22) | copy-start | bytes 196612
Sparse Core Ops, SparseCore 0:
  57.2 37.8 all-gather.2
  130.7 68.4 reduce-scatter.1
where the time goes:
time: 251 us; the launch traced here: 250 us
  waiting for transfers between devices  110 us (44%)
  blocking collectives  40.9 us (16%)
  matrix products  25.5 us (10%)
  starting transfers between devices  24.5 us (10%)
  local copies, waits for them, and re-layouts  17.5 us (7%)
  other arithmetic  16.8 us (7%)
  between operations  14.9 us (6%)
    reduce_scatter x1, waiting for transfers between devices, sum_packed(): lax.psum_scatter(lines, axis, tiled=True).reshape(-1)  68.7 us
    all_to_all x1, blocking collectives, summed_on_arrival(): lax.all_to_all(blocks, axis, split_axis=0, concat_axis=0, tiled=True)  24.9 us
    all_to_all x1, blocking collectives, sent_to_all(): lax.all_to_all(jnp.broadcast_to(array[None], (peers, *array.shape)), axis...  15.9 us
    dot_general x6, matrix products, one_block(): jnp.dot(weights, value_head, preferred_element_type=jnp.float32) / row_total  13.4 us
    reduce_sum x6, other arithmetic, one_block(): row_total = jnp.sum(exponent, axis=1, keepdims=True)  11.1 us
    all_to_all x1, waiting for transfers between devices, per_device(): lax.all_to_all(query_split, 'sp', split_axis=1, concat_axis=0, tiled=True)  11 us
    all_to_all x1, waiting for transfers between devices, per_device(): lax.all_to_all(key_split, 'sp', split_axis=1, concat_axis=0, tiled=True)  11 us
    all_to_all x1, waiting for transfers between devices, per_device(): lax.all_to_all(value_split, 'sp', split_axis=1, concat_axis=0, tiled=True)  10.5 us
  transfers between devices with their start and end apart: 6, of which 5 were waited for; matrix products, arithmetic and copies ran while one was open for 16% of the time, Pallas kernels for 0%

commit v1 on v0

--- a/solution.py
+++ b/solution.py
@@ -165,7 +165,9 @@
     value_part = lax.all_to_all(value_split, "sp", split_axis=1, concat_axis=0, tiled=True)
     per_head = jax.vmap(attend_head, in_axes=1, out_axes=1)
     mixed = per_head(query_part[:, 0], key_part[:, 0], value_part[:, 0])[:, None]
-    returned = lax.all_to_all(mixed, "sp", split_axis=0, concat_axis=1, tiled=True)
+    returned = jnp.concatenate(
+        lax.all_to_all(jnp.stack(jnp.split(mixed, lax.axis_size("sp"), axis=0)), "sp", 0, 0), axis=1
+    )
     attended = returned.reshape(tok_dev, inner)
     inner_all, outer_all = gather_packed(
         (adapter_in.astype(jnp.bfloat16), adapter_out.astype(jnp.bfloat16)), "sp", (0, 0)

time: 251 us -> 257 us (1.024)
  local copies, waits for them, and re-layouts: 17.5 us -> 25.7 us
    unnamed x27 -> x41, local copies, waits for them, and re-layouts: 3.66 us -> 11 us
  transfers between devices with their start and end apart: 6 -> 6, of which waited for: 5 -> 5; matrix products, arithmetic and copies ran while one was open for 16% -> 19% of each run, Pallas kernels for 0% -> 0%
where the time goes in v1:
time: 257 us
  waiting for transfers between devices  109 us (42%)
  blocking collectives  41.1 us (16%)
  local copies, waits for them, and re-layouts  25.7 us (10%)
  matrix products  25.5 us (10%)
  starting transfers between devices  24.5 us (10%)
  other arithmetic  15.6 us (6%)
  between operations  14.9 us (6%)
    reduce_scatter x1, waiting for transfers between devices, sum_packed(): lax.psum_scatter(lines, axis, tiled=True).reshape(-1)  68.4 us
    all_to_all x1, blocking collectives, summed_on_arrival(): lax.all_to_all(blocks, axis, split_axis=0, concat_axis=0, tiled=True)  25.1 us
    all_to_all x1, blocking collectives, sent_to_all(): lax.all_to_all(jnp.broadcast_to(array[None], (peers, *array.shape)), axis...  15.9 us
    dot_general x6, matrix products, one_block(): jnp.dot(weights, value_head, preferred_element_type=jnp.float32) / row_total  13.4 us
    reduce_sum x6, other arithmetic, one_block(): row_total = jnp.sum(exponent, axis=1, keepdims=True)  11.1 us
    all_to_all x1, waiting for transfers between devices, per_device(): lax.all_to_all(key_split, 'sp', split_axis=1, concat_axis=0, tiled=True)  11 us
    all_to_all x1, waiting for transfers between devices, per_device(): lax.all_to_all(query_split, 'sp', split_axis=1, concat_axis=0, tiled=True)  11 us
    unnamed x41, local copies, waits for them, and re-layouts  11 us
  transfers between devices with their start and end apart: 6, of which 5 were waited for; matrix products, arithmetic and copies ran while one was open for 19% of the time, Pallas kernels for 0%

profile of v1, /device:TPU:8, one launch (start us, length us, event | category | flops | bytes accessed | tf_op | source)
XLA Modules:
  0.0 256.7 jit_solution(5649822319099927018)
XLA Ops:
  7.2 1.4 copy.62
  8.5 1.1 copy.55
  9.7 9.4 %all-to-all-start = ((bf16[192,16,1,128]{3,0,2,1:T(8,128)(2,1)}), bf16[192,16,1,128]{3,0,2,1:T(8,128)(2,1)S(1)}, u32[]{:S(2)}, u32[]{:S(2)}) async-start(bf16[192,16,1,128]{3,0,2,1:T(8,128)(2,1)} %copy.55), calls=%async_computation | async-start | bytes 1572864 | tf_op jit(solution)/shard_map/all_to_all | solution.py:163
  19.2 1.1 copy.56
  20.3 11.0 %all-to-all-done = bf16[192,16,1,128]{3,0,2,1:T(8,128)(2,1)S(1)} async-done(((bf16[192,16,1,128]{3,0,2,1:T(8,128)(2,1)}), bf16[192,16,1,128]{3,0,2,1:T(8,128)(2,1)S(1)}, u32[]{:S(2)}, u32[]{:S(2)}) %all-to-all-start) | async-done | bytes 786464 | tf_op jit(solution)/shard_map/all_to_all | solution.py:163
  31.3 5.0 %all-to-all-start.1 = ((bf16[192,16,1,128]{3,0,2,1:T(8,128)(2,1)}), bf16[192,16,1,128]{3,0,2,1:T(8,128)(2,1)S(1)}, u32[]{:S(2)}, u32[]{:S(2)}) async-start(bf16[192,16,1,128]{3,0,2,1:T(8,128)(2,1)} %copy.56), calls=%async_computation.1 | async-start | bytes 1572864 | tf_op jit(solution)/shard_map/all_to_all | solution.py:164
  36.5 1.1 copy.57
  37.6 11.0 %all-to-all-done.1 = bf16[192,16,1,128]{3,0,2,1:T(8,128)(2,1)S(1)} async-done(((bf16[192,16,1,128]{3,0,2,1:T(8,128)(2,1)}), bf16[192,16,1,128]{3,0,2,1:T(8,128)(2,1)S(1)}, u32[]{:S(2)}, u32[]{:S(2)}) %all-to-all-start.1) | async-done | bytes 786464 | tf_op jit(solution)/shard_map/all_to_all | solution.py:164
  48.7 5.0 %all-to-all-start.2 = ((bf16[192,16,1,128]{3,0,2,1:T(8,128)(2,1)}), bf16[192,16,1,128]{3,0,2,1:T(8,128)(2,1)S(1)}, u32[]{:S(2)}, u32[]{:S(2)}) async-start(bf16[192,16,1,128]{3,0,2,1:T(8,128)(2,1)} %copy.57), calls=%async_computation.2 | async-start | bytes 1572864 | tf_op jit(solution)/shard_map/all_to_all | solution.py:165
  53.8 0.6 pad_maximum_fusion.2
  55.4 10.5 %all-to-all-done.2 = bf16[192,16,1,128]{3,0,2,1:T(8,128)(2,1)S(1)} async-done(((bf16[192,16,1,128]{3,0,2,1:T(8,128)(2,1)}), bf16[192,16,1,128]{3,0,2,1:T(8,128)(2,1)S(1)}, u32[]{:S(2)}, u32[]{:S(2)}) %all-to-all-start.2) | async-done | bytes 786464 | tf_op jit(solution)/shard_map/all_to_all | solution.py:165
  66.0 31.9 %while.10 = (s32[]{:T(128)}, bf16[6,1,512,128]{3,2,1,0:T(8,128)(2,1)S(1)}, s32[6,512]{1,0:T(8,128)S(1)}, s32[3072]{0:T(1024)S(1)}, bf16[6,1,512,128]{3,2,1,0:T(8...) while((s32[]{:T(128)}, ...), condition=%wide.region_5.6_spmd, body=%wide.region_2.5_spmd.sunk | while | flops 827456512 | bytes 20766816 | solution.py:155
  66.0 1.2 fusion.81
  67.2 1.9 fusion.82
  69.0 2.2 fusion.83
  71.3 1.2 fusion.81
  72.5 1.9 fusion.82
  74.3 2.2 fusion.83
  76.6 1.2 fusion.81
  77.8 1.9 fusion.82
  79.7 2.2 fusion.83
  81.9 1.2 fusion.81
  83.1 1.9 fusion.82
  85.0 2.2 fusion.83
  87.2 1.2 fusion.81
  88.4 1.9 fusion.82
  90.3 2.2 fusion.83
  92.5 1.2 fusion.81
  93.7 1.9 fusion.82
  95.6 2.2 fusion.83
  107.7 5.0 %all-to-all-start.3 = ((bf16[16,192,1,1,128]{4,1,3,2,0:T(8,128)(2,1)}), bf16[16,192,1,1,128]{4,1,3,2,0:T(8,128)(2,1)S(1)}, u32[]{:S(2)}, u32[]{:S(2)}) async-start(bf16[16,192,1,1,128]{4,1,3,2,0:T(8,128)(2,1)} %fusion.49), calls=%async_computation.3 | async-start | bytes 1572864 | tf_op jit(solution)/shard_map/all_to_all | solution.py:169
  112.9 1.7 reshape.151
  114.7 1.2 reshape_reshape.16
  115.9 1.0 reshape_reshape.18
  117.0 8.1 %all-to-all-done.3 = bf16[16,192,1,1,128]{4,1,3,2,0:T(8,128)(2,1)S(1)} async-done(((bf16[16,192,1,1,128]{4,1,3,2,0:T(8,128)(2,1)}), bf16[16,192,1,1,128]{4,1,3,2,0:T(8,128)(2,1)S(1)}, u32[]{:S(2)}, u32[]{:S(2)}) %all-to-all-start.3) | async-done | bytes 786464 | tf_op jit(solution)/shard_map/all_to_all | solution.py:169
  125.6 3.0 %convolution_multiply_fusion.1 = f32[2048,128]{1,0:T(8,128)S(1)} fusion(bf16[128,3072]{1,0:T(8,128)(2,1)} %reshape_reshape.16, bf16[1,192,3072]{2,1,0:T(8,128)(2,1)} %param.17, bf16[24,8,16,128]{3,2,1,0:T(8,128)(2,1)S(1)} %bitcast.166, bf16[192]{0:T(256)(128)(2,1)S(1)} %compare_convert_fusion), kind=kOutput, calls=%fused_computation.22 | convolution fusion | flops 252559360 | bytes 3801472 | tf_op jit(solution)/shard_map/dot_general | solution.py:106
  128.6 1.2 reshape_reshape.17
  129.8 2.0 convolution_multiply_fusion
  131.8 1.4 reshape_reshape.19
  133.2 1.9 pad_maximum_fusion
  135.1 1.7 reshape.148
  136.9 68.4 %reduce-scatter.2.cloned.1.call-done = f32[320,128]{1,0:T(8,128)} async-done(((f32[5120,128]{1,0:T(8,128)}), f32[320,128]{1,0:T(8,128)}) %reduce-scatter.2.cloned.1.call-update) | async-done | bytes 163856 | tf_op jit(solution)/shard_map/reduce_scatter | solution.py:44
  205.3 0.9 slice_bitcast_fusion
  206.2 0.8 slice_bitcast_fusion.1
  207.1 25.1 %all_to_all.65 = f32[32,1,1280]{2,1,0:T(1,128)S(1)} all-to-all(f32[32,1,1280]{2,1,0:T(1,128)S(1)} %bitcast.196), channel_id=1, replica_groups=mesh['rep'=32,'sp'=16] {'rep'}, dimensions={0} | all-to-all | bytes 327680 | tf_op jit(solution)/shard_map/all_to_all | solution.py:72
  232.4 15.9 %all_to_all.66 = f32[32,1,1280]{2,1,0:T(1,128)S(1)} all-to-all(f32[32,1,1280]{2,1,0:T(1,128)S(1)} %broadcast_in_dim.21), channel_id=1, replica_groups=mesh['rep'=32,'sp'=16] {'rep'}, dimensions={0} | all-to-all | bytes 327680 | tf_op jit(solution)/shard_map/all_to_all | solution.py:61
  248.4 0.7 multiply_add_fusion
  249.2 0.7 multiply_add_fusion.2
  (68 shorter events, 11.6 us)
Async XLA Ops:
  7.2 11.9 %copy-start.1 = (bf16[1,192,2048]{2,1,0:T(8,128)(2,1)S(1)}, bf16[1,192,2048]{2,1,0:T(8,128)(2,1)}, u32[]{:S(2)}) copy-start(bf16[1,192,2048]{2,1,0:T(8,128)(2,1)} %param.15) | copy-start | bytes 2359300
  9.7 26.7 %copy-start.2 = (bf16[1,192,2048]{2,1,0:T(8,128)(2,1)S(1)}, bf16[1,192,2048]{2,1,0:T(8,128)(2,1)}, u32[]{:S(2)}) copy-start(bf16[1,192,2048]{2,1,0:T(8,128)(2,1)} %param.16) | copy-start | bytes 2359300
  9.7 21.7 %all-to-all-start = ((bf16[192,16,1,128]{3,0,2,1:T(8,128)(2,1)}), bf16[192,16,1,128]{3,0,2,1:T(8,128)(2,1)S(1)}, u32[]{:S(2)}, u32[]{:S(2)}) async-start(bf16[192,16,1,128]{3,0,2,1:T(8,128)(2,1)} %copy.55), calls=%async_computation | async-start | bytes 1572864 | tf_op jit(solution)/shard_map/all_to_all | solution.py:163
  20.3 33.4 %copy-start.3 = (f32[8,3072]{1,0:T(8,128)S(1)}, f32[8,3072]{1,0:T(8,128)}, u32[]{:S(2)}) copy-start(f32[8,3072]{1,0:T(8,128)} %param.21) | copy-start | bytes 294916
  20.3 33.5 %copy-start.4 = (f32[128,128]{1,0:T(8,128)S(1)}, f32[128,128]{1,0:T(8,128)}, u32[]{:S(2)}) copy-start(f32[128,128]{1,0:T(8,128)} %param.20) | copy-start | bytes 196612
  20.3 34.8 %copy-start.10 = (s32[1,3]{1,0:T(1,128)S(1)}, s32[1,3]{1,0:T(1,128)}, u32[]{:S(2)}) copy-start(s32[1,3]{1,0:T(1,128)} %param.19) | copy-start | bytes 40
  31.3 17.3 %all-to-all-start.1 = ((bf16[192,16,1,128]{3,0,2,1:T(8,128)(2,1)}), bf16[192,16,1,128]{3,0,2,1:T(8,128)(2,1)S(1)}, u32[]{:S(2)}, u32[]{:S(2)}) async-start(bf16[192,16,1,128]{3,0,2,1:T(8,128)(2,1)} %copy.56), calls=%async_computation.1 | async-start | bytes 1572864 | tf_op jit(solution)/shard_map/all_to_all | solution.py:164
  48.7 17.3 %all-to-all-start.2 = ((bf16[192,16,1,128]{3,0,2,1:T(8,128)(2,1)}), bf16[192,16,1,128]{3,0,2,1:T(8,128)(2,1)S(1)}, u32[]{:S(2)}, u32[]{:S(2)}) async-start(bf16[192,16,1,128]{3,0,2,1:T(8,128)(2,1)} %copy.57), calls=%async_computation.2 | async-start | bytes 1572864 | tf_op jit(solution)/shard_map/all_to_all | solution.py:165
  53.7 59.2 %all-gather.3.cloned.1.call-start = ((), (), s32[]{:S(2)}) async-start(), calls=%async_computation.8 | async-start | bytes 1392640 | tf_op jit(solution)/shard_map/all_gather | solution.py:24
  107.7 17.3 %all-to-all-start.3 = ((bf16[16,192,1,1,128]{4,1,3,2,0:T(8,128)(2,1)}), bf16[16,192,1,1,128]{4,1,3,2,0:T(8,128)(2,1)S(1)}, u32[]{:S(2)}, u32[]{:S(2)}) async-start(bf16[16,192,1,1,128]{4,1,3,2,0:T(8,128)(2,1)} %fusion.49), calls=%async_computation.3 | async-start | bytes 1572864 | tf_op jit(solution)/shard_map/all_to_all | solution.py:169
  112.8 92.6 %reduce-scatter.2.cloned.1.call-start = ((), (), s32[]{:S(2)}) async-start(), calls=%async_computation.7 | async-start | bytes 2785280 | tf_op jit(solution)/shard_map/reduce_scatter | solution.py:44
  125.6 4.2 %copy-start = (bf16[2048,128]{1,0:T(8,128)(2,1)S(1)}, bf16[2048,128]{1,0:T(8,128)(2,1)}, u32[]{:S(2)}) copy-start(bf16[2048,128]{1,0:T(8,128)(2,1)} %reshape_reshape.18) | copy-start | bytes 1572868
  136.8 111.6 %copy-start.6 = (f32[8,3072]{1,0:T(8,128)S(1)}, f32[8,3072]{1,0:T(8,128)}, u32[]{:S(2)}) copy-start(f32[8,3072]{1,0:T(8,128)} %param.25) | copy-start | bytes 294916
  136.8 111.6 %copy-start.7 = (f32[8,3072]{1,0:T(8,128)S(1)}, f32[8,3072]{1,0:T(8,128)}, u32[]{:S(2)}) copy-start(f32[8,3072]{1,0:T(8,128)} %param.24) | copy-start | bytes 294916
  136.8 112.3 %copy-start.5 = (f32[128,128]{1,0:T(8,128)S(1)}, f32[128,128]{1,0:T(8,128)}, u32[]{:S(2)}) copy-start(f32[128,128]{1,0:T(8,128)} %param.20) | copy-start | bytes 196612
  136.8 112.3 %copy-start.8 = (f32[128,128]{1,0:T(8,128)S(1)}, f32[128,128]{1,0:T(8,128)}, u32[]{:S(2)}) copy-start(f32[128,128]{1,0:T(8,128)} %param.23) | copy-start | bytes 196612
  136.8 112.3 %copy-start.9 = (f32[128,128]{1,0:T(8,128)S(1)}, f32[128,128]{1,0:T(8,128)}, u32[]{:S(2)}) copy-start(f32[128,128]{1,0:T(8,128)} %param.22) | copy-start | bytes 196612
Sparse Core Ops, SparseCore 0:
  57.2 37.8 all-gather.2
  137.0 68.2 reduce-scatter.1
